TPU v7x, 32 devices: a whole 2x2x4 slice. The times are simulated.
32 devices in a mesh: group: 4 (over x, core), dp: 8 (over z, y).
Axes of the slice: x: 2, y: 2, z: 4, core: 2. Of those that a mesh axis runs over, the one named last changes fastest.
Arguments:
- images: float32 [64, 576, 768], P(('group', 'dp')), may hold values from -6 to 6
- cotangent: float32 [64, 576, 768], P(('group', 'dp')), may hold values from -6 to 6
- resolution: int32 [64], P(('group', 'dp')), may hold values from 0 to 2, as said below
- assignment: int32 [64], P(('group', 'dp')), may hold values from 0 to 3, as said below
- counts: int32 [4], replicated, may hold values from 1000 to 63999
- ln1_gain: float32 [768], P('dp'), may hold values from 0.25 to 1.75
- ln1_shift: float32 [768], P('dp'), may hold values from -3 to 3
- qkv_weight: float32 [768, 2304], P('dp'), may hold values from -0.21875 to 0.21875
- qkv_bias: float32 [2304], P('dp'), may hold values from -3 to 3
- rope_freqs: float32 [768], P('dp'), may hold values from -3 to 3
- out_weight: float32 [768, 768], P('dp'), may hold values from -1.75 to 1.75
- out_bias: float32 [768], P('dp'), may hold values from -3 to 3
- ln2_gain: float32 [768], P('dp'), may hold values from 0.25 to 1.75
- ln2_shift: float32 [768], P('dp'), may hold values from -3 to 3
- up_weight: float32 [768, 3072], P('dp'), may hold values from -0.21875 to 0.21875
- up_bias: float32 [3072], P('dp'), may hold values from -3 to 3
- down_weight: float32 [3072, 768], P('dp'), may hold values from -0.109375 to 0.109375
- down_bias: float32 [768], P('dp'), may hold values from -3 to 3
Outputs:
- activations: float32 [64, 576, 768], P(('group', 'dp'))
- input_grad: float32 [64, 576, 768], P(('group', 'dp'))
- grad_ln1_gain: float32 [768], P('dp')
- grad_ln1_shift: float32 [768], P('dp')
- grad_qkv_weight: float32 [768, 2304], P('dp')
- grad_qkv_bias: float32 [2304], P('dp')
- grad_rope_freqs: float32 [768], P('dp')
- grad_out_weight: float32 [768, 768], P('dp')
- grad_out_bias: float32 [768], P('dp')
- grad_ln2_gain: float32 [768], P('dp')
- grad_ln2_shift: float32 [768], P('dp')
- grad_up_weight: float32 [768, 3072], P('dp')
- grad_up_bias: float32 [3072], P('dp')
- grad_down_weight: float32 [3072, 768], P('dp')
- grad_down_bias: float32 [768], P('dp')
Inputs may be any that keep to these rules, and one draw needn't show every extreme that they name: resolution index 0, 1, 2 means 14, 20, 24 patches a side; the first image of each index of group has resolution equal to its group number mod 3, and the group's other images often do. `assignment`: all images on one index of group carry the same group number, and the 4 indices carry different ones.
All inputs are finite; a program needn't handle non-finite values.
Results may differ from a plain program's by a relative error of at most 0.015.
The roundings to bfloat16 on the way count: a program that leaves them out, or rounds other values in their place, can miss the bound.
Values may be sent and summed in bfloat16 or wider, within the bound.
A program may use at most 256 MiB of HBM per device.

v0:
```python
import math

import jax
import jax.numpy as jnp
from jax import lax
from jax.sharding import PartitionSpec as P

HEADS = 12
HD = 64
SIDE_S = 14
SIDE_M = 20
SIDE_L = 24
SLOT = 576


LN_EPS = 1e-06
MASK_FILL = -1e30


def norm_forward(values, gain, shift):
    average = jnp.mean(values, axis=-1, keepdims=True)
    centred = values - average
    variance = jnp.mean(centred * centred, axis=-1, keepdims=True)
    inv_std = lax.rsqrt(variance + LN_EPS)
    unit_rows = centred * inv_std
    return (unit_rows * gain + shift, unit_rows, inv_std)


def norm_backward(grad_rows, unit_rows, inv_std, gain):
    scaled = grad_rows * gain
    centre_term = jnp.mean(scaled, axis=-1, keepdims=True)
    slope_term = jnp.mean(scaled * unit_rows, axis=-1, keepdims=True)
    return inv_std * (scaled - centre_term - unit_rows * slope_term)


def rotate(values, cosine, sine):
    half_dim = values.shape[-1] // 2
    lower_half = values[..., :half_dim]
    upper_half = values[..., half_dim:]
    return jnp.concatenate(
        [lower_half * cosine - upper_half * sine, lower_half * sine + upper_half * cosine], axis=-1
    )


def unrotate(grads, rotated, cosine, sine):
    half_dim = grads.shape[-1] // 2
    grad_lower = grads[..., :half_dim]
    grad_upper = grads[..., half_dim:]
    rot_lower = rotated[..., :half_dim]
    rot_upper = rotated[..., half_dim:]
    back_rows = jnp.concatenate(
        [grad_lower * cosine + grad_upper * sine, grad_upper * cosine - grad_lower * sine], axis=-1
    )
    angle_grad = rot_lower * grad_upper - grad_lower * rot_upper
    return (back_rows, angle_grad)


def gelu_exact(values):
    return jax.nn.gelu(values, approximate=False)


def attend_forward(operands):
    query_rows, key_rows, value_rows, valid = operands
    factor = 1.0 / math.sqrt(query_rows.shape[-1])
    scores = (
        jnp.einsum("shd,thd->hst", query_rows, key_rows, preferred_element_type=jnp.float32)
        * factor
    )
    masked = jnp.where(valid[None, None, :], scores, MASK_FILL)
    row_top = jnp.max(masked, axis=-1, keepdims=True)
    log_total = row_top + jnp.log(jnp.sum(jnp.exp(masked - row_top), axis=-1, keepdims=True))
    probs_low = jnp.exp(masked - log_total).astype(jnp.bfloat16)
    context = jnp.einsum("hst,thd->shd", probs_low, value_rows, preferred_element_type=jnp.float32)
    return (context, log_total)


def attend_backward(operands):
    query_rows, key_rows, value_rows, valid, log_total, grad_context = operands
    factor = 1.0 / math.sqrt(query_rows.shape[-1])
    scores = (
        jnp.einsum("shd,thd->hst", query_rows, key_rows, preferred_element_type=jnp.float32)
        * factor
    )
    masked = jnp.where(valid[None, None, :], scores, MASK_FILL)
    probs = jnp.exp(masked - log_total)
    probs_low = probs.astype(jnp.bfloat16)
    grad_probs = jnp.einsum(
        "shd,thd->hst", grad_context, value_rows, preferred_element_type=jnp.float32
    )
    grad_values = jnp.einsum(
        "hst,shd->thd", probs_low, grad_context, preferred_element_type=jnp.float32
    )
    grad_scores = probs * (grad_probs - jnp.sum(probs * grad_probs, axis=-1, keepdims=True))
    scores_low = grad_scores.astype(jnp.bfloat16)
    grad_query = (
        jnp.einsum("hst,thd->shd", scores_low, key_rows, preferred_element_type=jnp.float32)
        * factor
    )
    grad_key = (
        jnp.einsum("hst,shd->thd", scores_low, query_rows, preferred_element_type=jnp.float32)
        * factor
    )
    return (grad_query, grad_key, grad_values)


def weighted_outer(device_weight, left_rows, right_rows):
    return device_weight * jnp.einsum(
        "isd,isf->df", left_rows, right_rows, preferred_element_type=jnp.float32
    )


def weighted_rows(device_weight, values):
    return device_weight * jnp.sum(values.astype(jnp.float32), axis=(0, 1))


def on_device(
    images,
    cotangent,
    resolution,
    assignment,
    counts,
    ln1_gain,
    ln1_shift,
    qkv_weight,
    qkv_bias,
    rope_freqs,
    out_weight,
    out_bias,
    ln2_gain,
    ln2_shift,
    up_weight,
    up_bias,
    down_weight,
    down_bias,
):
    bf16 = jnp.bfloat16
    f32 = jnp.float32
    copies = (
        lax.all_gather(ln1_gain.astype(bf16), "dp", axis=0, tiled=True),
        lax.all_gather(ln1_shift.astype(bf16), "dp", axis=0, tiled=True),
        lax.all_gather(qkv_weight.astype(bf16), "dp", axis=0, tiled=True),
        lax.all_gather(qkv_bias.astype(bf16), "dp", axis=0, tiled=True),
        lax.all_gather(rope_freqs.astype(bf16), "dp", axis=0, tiled=True),
        lax.all_gather(out_weight.astype(bf16), "dp", axis=0, tiled=True),
        lax.all_gather(out_bias.astype(bf16), "dp", axis=0, tiled=True),
        lax.all_gather(ln2_gain.astype(bf16), "dp", axis=0, tiled=True),
        lax.all_gather(ln2_shift.astype(bf16), "dp", axis=0, tiled=True),
        lax.all_gather(up_weight.astype(bf16), "dp", axis=0, tiled=True),
        lax.all_gather(up_bias.astype(bf16), "dp", axis=0, tiled=True),
        lax.all_gather(down_weight.astype(bf16), "dp", axis=0, tiled=True),
        lax.all_gather(down_bias.astype(bf16), "dp", axis=0, tiled=True),
    )
    gain_one = copies[0].astype(f32)
    shift_one = copies[1].astype(f32)
    weight_qkv = copies[2]
    bias_qkv = copies[3].astype(f32)
    freq_table = copies[4].astype(f32).reshape(2, HEADS, HD // 2)
    weight_out = copies[5]
    bias_out = copies[6].astype(f32)
    gain_two = copies[7].astype(f32)
    shift_two = copies[8].astype(f32)
    weight_up = copies[9]
    bias_up = copies[10].astype(f32)
    weight_down = copies[11]
    bias_down = copies[12].astype(f32)
    image_count = images.shape[0]
    model_dim = images.shape[-1]
    head_shape = (image_count, SLOT, HEADS, HD)
    side_len = jnp.where(
        resolution == 0, SIDE_S, jnp.where(resolution == 1, SIDE_M, SIDE_L)
    ).astype(jnp.int32)
    positions = jnp.arange(SLOT, dtype=jnp.int32)
    column = (positions[None, :] % side_len[:, None]).astype(f32)
    row_pos = (positions[None, :] // side_len[:, None]).astype(f32)
    valid = positions[None, :] < (side_len * side_len)[:, None]
    group_total = counts.shape[0]
    counts_float = counts.astype(f32)
    matches = assignment[0] == jnp.arange(group_total, dtype=jnp.int32)
    picked = jnp.sum(jnp.where(matches, counts_float, 0.0))
    device_weight = (
        group_total
        * picked
        / jnp.sum(counts_float)
        / math.sqrt(lax.axis_size("dp") * image_count * SLOT)
    )
    normed_one, unit_one, inv_one = norm_forward(images, gain_one, shift_one)
    normed_one = normed_one.astype(bf16)
    projected = (
        jnp.einsum("isd,df->isf", normed_one, weight_qkv, preferred_element_type=f32) + bias_qkv
    )
    angle = column[:, :, None, None] * freq_table[0] + row_pos[:, :, None, None] * freq_table[1]
    cosine = jnp.cos(angle)
    sine = jnp.sin(angle)
    query_rot = rotate(projected[..., :model_dim].reshape(head_shape), cosine, sine)
    key_rot = rotate(projected[..., model_dim : 2 * model_dim].reshape(head_shape), cosine, sine)
    query_rows = query_rot.astype(bf16)
    key_rows = key_rot.astype(bf16)
    value_rows = projected[..., 2 * model_dim :].reshape(head_shape).astype(bf16)
    context, log_total = lax.map(attend_forward, (query_rows, key_rows, value_rows, valid))
    context_low = context.reshape(image_count, SLOT, model_dim).astype(bf16)
    attended = (
        jnp.einsum("isd,de->ise", context_low, weight_out, preferred_element_type=f32) + bias_out
    )
    middle = images + attended
    normed_two, unit_two, inv_two = norm_forward(middle, gain_two, shift_two)
    normed_two = normed_two.astype(bf16)
    hidden_pre = (
        jnp.einsum("isd,df->isf", normed_two, weight_up, preferred_element_type=f32) + bias_up
    )
    gelu_value, gelu_pull = jax.vjp(gelu_exact, hidden_pre)
    hidden = gelu_value.astype(bf16)
    branch = jnp.einsum("isf,fd->isd", hidden, weight_down, preferred_element_type=f32) + bias_down
    activations = jnp.where(valid[:, :, None], middle + branch, 0.0)
    grad_branch = jnp.where(valid[:, :, None], cotangent, 0.0)
    branch_low = grad_branch.astype(bf16)
    grad_down_w = weighted_outer(device_weight, hidden, branch_low)
    grad_down_b = weighted_rows(device_weight, branch_low)
    grad_hidden = jnp.einsum("isd,fd->isf", branch_low, weight_down, preferred_element_type=f32)
    grad_pre = gelu_pull(grad_hidden)[0].astype(bf16)
    grad_up_w = weighted_outer(device_weight, normed_two, grad_pre)
    grad_up_b = weighted_rows(device_weight, grad_pre)
    grad_normed_two = jnp.einsum("isf,df->isd", grad_pre, weight_up, preferred_element_type=f32)
    grad_gain_two = weighted_rows(device_weight, grad_normed_two * unit_two)
    grad_shift_two = weighted_rows(device_weight, grad_normed_two)
    grad_middle = grad_branch + norm_backward(grad_normed_two, unit_two, inv_two, gain_two)
    attended_low = grad_middle.astype(bf16)
    grad_out_w = weighted_outer(device_weight, context_low, attended_low)
    grad_out_b = weighted_rows(device_weight, attended_low)
    grad_context = (
        jnp.einsum("ise,de->isd", attended_low, weight_out, preferred_element_type=f32)
        .astype(bf16)
        .reshape(head_shape)
    )
    grad_query, grad_key, grad_value = lax.map(
        attend_backward, (query_rows, key_rows, value_rows, valid, log_total, grad_context)
    )
    query_back, query_angle = unrotate(grad_query, query_rot, cosine, sine)
    key_back, key_angle = unrotate(grad_key, key_rot, cosine, sine)
    angle_sum = query_angle + key_angle
    grad_freq_col = device_weight * jnp.sum(angle_sum * column[:, :, None, None], axis=(0, 1))
    grad_freq_row = device_weight * jnp.sum(angle_sum * row_pos[:, :, None, None], axis=(0, 1))
    grad_freqs = jnp.stack([grad_freq_col, grad_freq_row]).reshape(-1)
    flat_shape = (image_count, SLOT, model_dim)
    grad_projected = jnp.concatenate(
        [
            query_back.reshape(flat_shape),
            key_back.reshape(flat_shape),
            grad_value.reshape(flat_shape),
        ],
        axis=-1,
    ).astype(bf16)
    grad_qkv_w = weighted_outer(device_weight, normed_one, grad_projected)
    grad_qkv_b = weighted_rows(device_weight, grad_projected)
    grad_normed_one = jnp.einsum(
        "isf,df->isd", grad_projected, weight_qkv, preferred_element_type=f32
    )
    grad_gain_one = weighted_rows(device_weight, grad_normed_one * unit_one)
    grad_shift_one = weighted_rows(device_weight, grad_normed_one)
    input_grad = grad_middle + norm_backward(grad_normed_one, unit_one, inv_one, gain_one)
    grads = (
        grad_gain_one,
        grad_shift_one,
        grad_qkv_w,
        grad_qkv_b,
        grad_freqs,
        grad_out_w,
        grad_out_b,
        grad_gain_two,
        grad_shift_two,
        grad_up_w,
        grad_up_b,
        grad_down_w,
        grad_down_b,
    )
    shards = (
        lax.psum_scatter(grads[0], "dp", scatter_dimension=0, tiled=True),
        lax.psum_scatter(grads[1], "dp", scatter_dimension=0, tiled=True),
        lax.psum_scatter(grads[2], "dp", scatter_dimension=0, tiled=True),
        lax.psum_scatter(grads[3], "dp", scatter_dimension=0, tiled=True),
        lax.psum_scatter(grads[4], "dp", scatter_dimension=0, tiled=True),
        lax.psum_scatter(grads[5], "dp", scatter_dimension=0, tiled=True),
        lax.psum_scatter(grads[6], "dp", scatter_dimension=0, tiled=True),
        lax.psum_scatter(grads[7], "dp", scatter_dimension=0, tiled=True),
        lax.psum_scatter(grads[8], "dp", scatter_dimension=0, tiled=True),
        lax.psum_scatter(grads[9], "dp", scatter_dimension=0, tiled=True),
        lax.psum_scatter(grads[10], "dp", scatter_dimension=0, tiled=True),
        lax.psum_scatter(grads[11], "dp", scatter_dimension=0, tiled=True),
        lax.psum_scatter(grads[12], "dp", scatter_dimension=0, tiled=True),
    )
    reduced = (
        lax.psum(shards[0].astype(jnp.bfloat16), "group").astype(jnp.float32),
        lax.psum(shards[1].astype(jnp.bfloat16), "group").astype(jnp.float32),
        lax.psum(shards[2].astype(jnp.bfloat16), "group").astype(jnp.float32),
        lax.psum(shards[3].astype(jnp.bfloat16), "group").astype(jnp.float32),
        lax.psum(shards[4].astype(jnp.bfloat16), "group").astype(jnp.float32),
        lax.psum(shards[5].astype(jnp.bfloat16), "group").astype(jnp.float32),
        lax.psum(shards[6].astype(jnp.bfloat16), "group").astype(jnp.float32),
        lax.psum(shards[7].astype(jnp.bfloat16), "group").astype(jnp.float32),
        lax.psum(shards[8].astype(jnp.bfloat16), "group").astype(jnp.float32),
        lax.psum(shards[9].astype(jnp.bfloat16), "group").astype(jnp.float32),
        lax.psum(shards[10].astype(jnp.bfloat16), "group").astype(jnp.float32),
        lax.psum(shards[11].astype(jnp.bfloat16), "group").astype(jnp.float32),
        lax.psum(shards[12].astype(jnp.bfloat16), "group").astype(jnp.float32),
    )
    return (
        activations,
        input_grad,
        reduced[0],
        reduced[1],
        reduced[2],
        reduced[3],
        reduced[4],
        reduced[5],
        reduced[6],
        reduced[7],
        reduced[8],
        reduced[9],
        reduced[10],
        reduced[11],
        reduced[12],
    )


def solution(mesh):
    placed = (
        P(("group", "dp"), None, None),
        P(("group", "dp"), None, None),
        P(("group", "dp")),
        P(("group", "dp")),
        P(),
        P("dp"),
        P("dp"),
        P("dp", None),
        P("dp"),
        P("dp"),
        P("dp", None),
        P("dp"),
        P("dp"),
        P("dp"),
        P("dp", None),
        P("dp"),
        P("dp", None),
        P("dp"),
    )
    return jax.shard_map(
        on_device,
        mesh=mesh,
        in_specs=placed,
        out_specs=(
            P(("group", "dp"), None, None),
            P(("group", "dp"), None, None),
            P("dp"),
            P("dp"),
            P("dp", None),
            P("dp"),
            P("dp"),
            P("dp", None),
            P("dp"),
            P("dp"),
            P("dp"),
            P("dp", None),
            P("dp"),
            P("dp", None),
            P("dp"),
        ),
        check_vma=False,
    )
```

profile of v0, /device:TPU:0, one launch (start us, length us, event | category | flops | bytes accessed | tf_op | source)
XLA Modules:
  0.0 1047.0 jit_solution(3535258049018020494)
XLA Ops:
  43.9 40.8 %all-reduce.18 = (bf16[2304]{0:T(1024)(128)(2,1)}, bf16[768]{0:T(1024)(128)(2,1)}, bf16[768]{0:T(1024)(128)(2,1)}, bf16[768]{0:T(1024)(128)(2,1)}, bf16[768]{0:T...) all-reduce(bf16[2304]{0:T(1024)(128)(2,1)S(1)} %dynamic-update-slic, ...), channel_id=1, replica_groups=mesh['group'=4,'dp'=8] {'dp'}, use_global_device_ids=true, to_apply=%add.2 | all-reduce | flops 7680 | bytes 30720
  95.7 26.1 %all-gather = bf16[8,1,384]{2,1,0:T(2,128)(2,1)S(1)} all-gather(bf16[1,1,384]{2,1,0:T(2,128)(2,1)} %reshape.355), channel_id=1, replica_groups=mesh['group'=4,'dp'=8] {'dp'}, dimensions={0}, use_global_device_ids=true | all-gather | bytes 6912 | tf_op jit(solution)/shard_map/all_gather | solution.py:149
  157.4 12.4 %fusion.74 = (bf16[2,576,12,32]{1,3,2,0:T(8,128)(2,1)S(1)}, bf16[2,576,12,32]{1,3,2,0:T(8,128)(2,1)S(1)}, bf16[2,576,12,32]{1,3,2,0:T(8,128)(2,1)S(1)}, bf16[2,576,12,32]{1,3,2,0:T(8,128)(2,1)S(1)}) fusion(f32[2,576,12,64]{1,3,2,0:T(8,128)} %bitcast.177, f32[12,32]{1,0:T(8,128)} %slice.71, f32[2,576]{1,0:T(2,128)} %get-tuple-element.250, ...), kind=kLoop, calls=%fused_computation.181 | loop fusion | flops 8404992 | bytes 10629120 | tf_op jit(solution)/shard_map/convert.11
  171.7 65.6 %while.28 = (s32[]{:T(128)}, bf16[2,576,12,64]{1,3,2,0:T(8,128)(2,1)}, f32[2,12,576,1]{2,1,3,0:T(8,128)S(1)}, bf16[2,576,12,64]{1,3,2,0:T(8,128)(2,1)}, pred[2,5...) while((s32[]{:T(128)}, ...), condition=%wide.region_5.6_spmd.clone, body=%wide.region_2.5_spmd.sunk.clone | while | flops 1063003392 | bytes 54543708 | solution.py:199
  193.0 11.4 %bitcast_dynamic-update-slice_fusion.16 = bf16[2,576,12,64]{1,3,2,0:T(8,128)(2,1)} fusion(bf16[2,576,12,64]{1,3,2,0:T(8,128)(2,1)} %get-tuple-element.419, s32[]{:T(128)S(6)} %copy.97, f32[12,576,576]{1,2,0:T(8,128)} %get-tuple-element.375, f32[12,576]{1,0:T(8,128)S(1)} %get-tuple-element.377, ...), kind=kOutput, calls=%fused_computation.6.clone.1.clone | convolution fusion | flops 525533184 | bytes 20476480 | tf_op jit(solution)/shard_map/while/body/eval_jaxpr/hst,thd->shd/dot_general | solution.py:73
  204.3 11.4 %fusion.116 = (f32[12,576]{1,0:T(8,128)S(1)}, f32[12,576,576]{1,2,0:T(8,128)}) fusion(pred[576]{0:T(1024)(128)(4,1)S(1)} %dynamic-slice_reduce_fusion.6, bf16[2,576,12,64]{1,3,2,0:T(8,128)(2,1)S(1)} %get-tuple-element.431, s32[]{:T(128)S(6)} %copy.97, bf16[2,576,12,64]{1,3,2,0:T(8,128)(2,1)} %get-tuple-element.430), kind=kOutput, calls=%fused_computation.3.clone.1.clone | convolution fusion | flops 521544960 | bytes 17921024 | tf_op jit(solution)/shard_map/while/body/eval_jaxpr/shd,thd->hst/dot_general | solution.py:66
  225.6 11.4 %bitcast_dynamic-update-slice_fusion.16 = bf16[2,576,12,64]{1,3,2,0:T(8,128)(2,1)} fusion(bf16[2,576,12,64]{1,3,2,0:T(8,128)(2,1)} %get-tuple-element.419, s32[]{:T(128)S(6)} %copy.97, f32[12,576,576]{1,2,0:T(8,128)} %get-tuple-element.375, f32[12,576]{1,0:T(8,128)S(1)} %get-tuple-element.377, ...), kind=kOutput, calls=%fused_computation.6.clone.1.clone | convolution fusion | flops 525533184 | bytes 20476480 | tf_op jit(solution)/shard_map/while/body/eval_jaxpr/hst,thd->shd/dot_general | solution.py:73
  244.7 17.1 %fusion.60 = (u8[576,3072]{1,0:T(8,128)(4,1)S(1)}, u8[576,3072]{1,0:T(8,128)(4,1)S(1)}, f32[2,576,3072]{2,1,0:T(8,128)}) fusion(f32[3072]{0:T(1024)S(1)} %bitcast.190, bf16[768,3072]{1,0:T(8,128)(2,1)} %all-gather.10.cloned.1.call-done, f32[2,576,768]{2,1,0:T(8,128)} %copy-done.10, f32[768]{0:T(1024)S(1)} %copy-done.43, f32[768]{0:T(1024)S(1)} %copy-done.37, ...), kind=kOutput, calls=%fused_computation.109 | convolution fusion | flops 5486247936 | bytes 25979904 | tf_op jit(solution)/shard_map/isd,df->isf/dot_general | solution.py:208
  261.8 35.6 %multiply_convert_fusion.1 = (bf16[2,576,3072]{2,1,0:T(8,128)(2,1)}, f32[2,576,3072]{2,1,0:T(8,128)}) fusion(f32[2,576,3072]{2,1,0:T(8,128)} %get-tuple-element.244, f32[3072]{0:T(1024)S(1)} %bitcast.191, u8[576,3072]{1,0:T(8,128)(4,1)S(1)} %get-tuple-element.130, u8[576,3072]{1,0:T(8,128)(4,1)S(1)} %get-tuple-element.129), kind=kLoop, calls=%fused_computation.64 | loop fusion | flops 251265024 | bytes 38940672 | tf_op jit(solution)/shard_map/convert_element_type | solution.py:211
  297.4 21.1 %convert_reduce_fusion = (f32[3072]{0:T(1024)}, bf16[2,576,3072]{2,1,0:T(8,128)(2,1)}) fusion(f32[2,576,3072]{2,1,0:T(8,128)} %get-tuple-element.214, bf16[2,576,768]{2,1,0:T(8,128)(2,1)} %get-tuple-element.210, bf16[3072,768]{1,0:T(8,128)(2,1)} %all-gather.12.cloned.1.call-done, f32[2,576,3072]{2,1,0:T(8,128)} %get-tuple-element.244, f32[3072]{0:T(1024)S(1)} %bitcast.192), kind=kOutput, calls=%fused_computation.62 | convolution fusion | flops 5495976960 | bytes 41902080 | tf_op jit(solution)/shard_map/isd,fd->isf/dot_general | solution.py:218
  318.5 11.3 %multiply_reduce_fusion.1 = (f32[768]{0:T(1024)}, f32[2,576]{1,0:T(2,128)S(1)}, f32[2,576]{1,0:T(2,128)S(1)}, f32[768]{0:T(1024)}, f32[2,576,768]{2,1,0:T(8,128)S(1)}) fusion(f32[2,576,768]{2,1,0:T(8,128)} %copy-done.10, f32[2,576]{1,0:T(2,128)S(1)} %add_rsqrt_fusion, f32[2,576]{1,0:T(2,128)S(1)} %broadcast_multiply_fusion.6, f32[768]{0:T(1024)S(1)} %copy-done.37, ...), kind=kOutput, calls=%fused_computation.95 | convolution fusion | flops 5443776512 | bytes 18902016 | tf_op jit(solution)/shard_map/isf,df->isd/dot_general | solution.py:222
  345.7 109.5 %while.29 = (s32[]{:T(128)}, f32[2,576,12,64]{1,3,2,0:T(8,128)}, f32[2,576,12,64]{1,3,2,0:T(8,128)}, bf16[2,576,12,64]{1,3,2,0:T(8,128)(2,1)}, bf16[2,576,12,64]...) while((s32[]{:T(128)}, f32[2,576,12,64]{1,3,2,0:T(8,128)}, ...), condition=%wide.region_12.13_spmd.clone, body=%wide.region_10.12_spmd.sunk.clone | while | flops 2608637184 | bytes 226033728 | solution.py:234
  366.7 13.3 %multiply_reduce_fusion.13 = (f32[12,576]{1,0:T(8,128)S(1)}, f32[12,576,576]{1,2,0:T(8,128)}) fusion(f32[12,576,576]{1,2,0:T(8,128)} %fusion.125, f32[12,576]{1,0:T(8,128)S(1)} %dynamic-slice_bitcast_fusion.3, pred[576]{0:T(1024)(128)(4,1)S(1)} %dynamic-slice_reduce_fusion.7, bf16[2,576,12,64]{1,3,2,0:T(8,128)(2,1)S(1)} %copy-done.3, ...), kind=kOutput, calls=%fused_computation.22.clone.1.clone | convolution fusion | flops 529507584 | bytes 33887232 | tf_op jit(solution)/shard_map/while/body/eval_jaxpr/shd,thd->hst/dot_general | solution.py:87
  380.0 14.3 %multiply_convert_fusion.4 = bf16[12,576,576]{1,2,0:T(8,128)(2,1)S(1)} fusion(f32[12,576,576]{1,2,0:T(8,128)} %get-tuple-element.398, f32[12,576,576]{1,2,0:T(8,128)} %fusion.125, f32[12,576]{1,0:T(8,128)S(1)} %get-tuple-element.399, f32[12,576]{1,0:T(8,128)S(1)} %dynamic-slice_bitcast_fusion.3, pred[576]{0:T(1024)(128)(4,1)S(1)} %dynamic-slice_reduce_fusion.7), kind=kLoop, calls=%fused_computation.21.clone.1.clone | loop fusion | flops 23887872 | bytes 39868992 | tf_op jit(solution)/shard_map/while/body/eval_jaxpr/convert_element_type | solution.py:94
  421.2 13.3 %multiply_reduce_fusion.13 = (f32[12,576]{1,0:T(8,128)S(1)}, f32[12,576,576]{1,2,0:T(8,128)}) fusion(f32[12,576,576]{1,2,0:T(8,128)} %fusion.125, f32[12,576]{1,0:T(8,128)S(1)} %dynamic-slice_bitcast_fusion.3, pred[576]{0:T(1024)(128)(4,1)S(1)} %dynamic-slice_reduce_fusion.7, bf16[2,576,12,64]{1,3,2,0:T(8,128)(2,1)S(1)} %copy-done.3, ...), kind=kOutput, calls=%fused_computation.22.clone.1.clone | convolution fusion | flops 529507584 | bytes 33887232 | tf_op jit(solution)/shard_map/while/body/eval_jaxpr/shd,thd->hst/dot_general | solution.py:87
  434.5 14.0 %multiply_convert_fusion.4 = bf16[12,576,576]{1,2,0:T(8,128)(2,1)S(1)} fusion(f32[12,576,576]{1,2,0:T(8,128)} %get-tuple-element.398, f32[12,576,576]{1,2,0:T(8,128)} %fusion.125, f32[12,576]{1,0:T(8,128)S(1)} %get-tuple-element.399, f32[12,576]{1,0:T(8,128)S(1)} %dynamic-slice_bitcast_fusion.3, pred[576]{0:T(1024)(128)(4,1)S(1)} %dynamic-slice_reduce_fusion.7), kind=kLoop, calls=%fused_computation.21.clone.1.clone | loop fusion | flops 23887872 | bytes 39868992 | tf_op jit(solution)/shard_map/while/body/eval_jaxpr/convert_element_type | solution.py:94
  459.3 15.3 %subtract_add_fusion = (f32[2,576,12,32]{1,3,2,0:T(8,128)S(1)}, bf16[2,576,12,32]{1,3,2,0:T(8,128)(2,1)}, bf16[2,576,12,32]{1,3,2,0:T(8,128)(2,1)}, bf16[2,576,12,32]{1,3,2,0:T(8,128)(2,1)S(1)}) fusion(f32[2,576,12,64]{1,3,2,0:T(8,128)} %get-tuple-element.110, f32[2,576,12,64]{1,3,2,0:T(8,128)} %get-tuple-element.109, f32[2,576,12,64]{1,3,2,0:T(8,128)} %bitcast.180, ...), kind=kLoop, calls=%fused_computation.122 | loop fusion | flops 15040512 | bytes 18591744 | tf_op jit(solution)/shard_map/add | solution.py:239
  504.1 12.6 %bitcast_multiply_fusion.1 = f32[768,3072]{1,0:T(8,128)} fusion(bf16[2,576,3072]{2,1,0:T(8,128)(2,1)} %get-tuple-element.248, f32[]{:T(128)S(6)} %div.60, f32[2,576,768]{2,1,0:T(8,128)} %copy-done.10, f32[768]{0:T(1024)} %convert_element_type.237, f32[768]{0:T(1024)S(1)} %copy-done.38, f32[2,576]{1,0:T(2,128)} %copy-done.34, f32[2,576]{1,0:T(2,128)} %copy-done.31), kind=kOutput, calls=%fused_computation.79 | convolution fusion | flops 5442600960 | bytes 20069380 | tf_op jit(solution)/shard_map/isd,isf->df/dot_general | solution.py:107
  516.8 11.5 %bitcast_multiply_fusion = f32[3072,768]{1,0:T(8,128)} fusion(bf16[2,576,3072]{2,1,0:T(8,128)(2,1)} %get-tuple-element.213, bf16[2,576,768]{2,1,0:T(8,128)(2,1)} %get-tuple-element.210, f32[]{:T(128)S(6)} %div.60), kind=kOutput, calls=%fused_computation.78 | convolution fusion | flops 5438177280 | bytes 18284548 | tf_op jit(solution)/shard_map/isd,isf->df/dot_general | solution.py:107
  535.6 11.3 %multiply_reduce_fusion.2 = (f32[768]{0:T(1024)S(1)}, f32[2,576]{1,0:T(2,128)S(1)}, f32[2,576]{1,0:T(2,128)}, f32[768]{0:T(1024)S(1)}, f32[2,576,768]{2,1,0:T(8,128)}) fusion(f32[2,576,768]{2,1,0:T(8,128)S(1)} %copy-done.2, f32[2,576]{1,0:T(2,128)} %add_rsqrt_fusion.1, f32[2,576]{1,0:T(2,128)S(1)} %copy-done.30, f32[768]{0:T(1024)} %convert_element_type.217, ...), kind=kOutput, calls=%fused_computation.97 | convolution fusion | flops 4100747520 | bytes 15952896 | tf_op jit(solution)/shard_map/isf,df->isd/dot_general | solution.py:254
  561.4 68.5 %reduce-scatter.5.cloned.1.call-done = f32[96,2304]{1,0:T(8,128)} async-done(((f32[768,2304]{1,0:T(8,128)}), f32[96,2304]{1,0:T(8,128)}) %reduce-scatter.5.cloned.1.call-update) | async-done | bytes 884752 | tf_op jit(solution)/shard_map/reduce_scatter | solution.py:278
  631.9 164.6 %reduce-scatter.9.cloned.1.call-done = f32[96,3072]{1,0:T(8,128)} async-done(((f32[768,3072]{1,0:T(8,128)}), f32[96,3072]{1,0:T(8,128)}) %reduce-scatter.9.cloned.1.call-update) | async-done | bytes 1179664 | tf_op jit(solution)/shard_map/reduce_scatter | solution.py:285
  798.7 164.5 %reduce-scatter.11.cloned.1.call-done = f32[384,768]{1,0:T(8,128)} async-done(((f32[3072,768]{1,0:T(8,128)}), f32[384,768]{1,0:T(8,128)}) %reduce-scatter.11.cloned.1.call-update) | async-done | bytes 1179664 | tf_op jit(solution)/shard_map/reduce_scatter | solution.py:287
  966.8 36.7 %all-reduce.17 = (bf16[768]{0:T(1024)(128)(2,1)}, bf16[768]{0:T(1024)(128)(2,1)}, bf16[2304]{0:T(1024)(128)(2,1)}, bf16[768]{0:T(1024)(128)(2,1)}, bf16[768]{0:T...) all-reduce(f32[768]{0:T(1024)} %broadcast_multiply_fusion.13, ...), channel_id=2, replica_groups=mesh['group'=4,'dp'=8] {'dp'}, use_global_device_ids=true, to_apply=%region_18.19.clone | all-reduce | flops 10752 | bytes 64512
  (298 shorter events, 287.7 us)
Async XLA Ops:
  7.2 127.5 %all-gather.6.cloned.1.call-start = ((), (), s32[]{:S(2)}) async-start(), calls=%async_computation.4 | async-start | bytes 3981312 | tf_op jit(solution)/shard_map/all_gather | solution.py:141
  9.2 228.2 %all-gather.8.cloned.1.call-start = ((), (), s32[]{:S(2)}) async-start(), calls=%async_computation.5 | async-start | bytes 1327104 | tf_op jit(solution)/shard_map/all_gather | solution.py:144
  10.9 16.3 %copy-start.46 = (f32[288]{0:T(512)S(1)}, f32[288]{0:T(512)}, u32[]{:S(2)}) copy-start(f32[288]{0:T(512)} %param.30) | copy-start | bytes 3460
  10.9 16.9 %copy-start.47 = (f32[384]{0:T(512)S(1)}, f32[384]{0:T(512)}, u32[]{:S(2)}) copy-start(f32[384]{0:T(512)} %param.37) | copy-start | bytes 4612
  10.9 19.3 %copy-start.1 = (f32[2,576,768]{2,1,0:T(8,128)S(1)}, f32[2,576,768]{2,1,0:T(8,128)}, u32[]{:S(2)}) copy-start(f32[2,576,768]{2,1,0:T(8,128)} %param.22) | copy-start | bytes 10616836
  11.0 233.7 %all-gather.10.cloned.1.call-start = ((), (), s32[]{:S(2)}) async-start(), calls=%async_computation.6 | async-start | bytes 5308416 | tf_op jit(solution)/shard_map/all_gather | solution.py:148
  13.3 284.0 %all-gather.12.cloned.1.call-start = ((), (), s32[]{:S(2)}) async-start(), calls=%async_computation.7 | async-start | bytes 5308416 | tf_op jit(solution)/shard_map/all_gather | solution.py:150
  15.6 544.2 %reduce-scatter.7.cloned.1.call-start = ((), (), s32[]{:S(2)}) async-start(), calls=%async_computation.9 | async-start | bytes 2654208 | tf_op jit(solution)/shard_map/reduce_scatter | solution.py:281
  93.1 64.3 %copy-start.23 = (f32[12,32]{1,0:T(8,128)}, f32[12,32]{1,0:T(8,128)S(1)}, u32[]{:S(2)}) copy-start(f32[12,32]{1,0:T(8,128)S(1)} %slice.69) | copy-start | bytes 4612
  171.7 65.7 %copy-start.44 = (f32[768]{0:T(1024)S(1)}, f32[768]{0:T(1024)}, u32[]{:S(2)}) copy-start(f32[768]{0:T(1024)} %convert_element_type.233) | copy-start | bytes 9220
  242.3 87.5 %copy-start.31 = (f32[2,576]{1,0:T(2,128)}, f32[2,576]{1,0:T(2,128)S(1)}, u32[]{:S(2)}) copy-start(f32[2,576]{1,0:T(2,128)S(1)} %broadcast_multiply_fusion.6) | copy-start | bytes 13828
  244.6 85.2 %copy-start.34 = (f32[2,576]{1,0:T(2,128)}, f32[2,576]{1,0:T(2,128)S(1)}, u32[]{:S(2)}) copy-start(f32[2,576]{1,0:T(2,128)S(1)} %add_rsqrt_fusion) | copy-start | bytes 13828
  336.9 293.1 %reduce-scatter.5.cloned.1.call-start = ((), (), s32[]{:S(2)}) async-start(), calls=%async_computation.8 | async-start | bytes 7962624 | tf_op jit(solution)/shard_map/reduce_scatter | solution.py:278
  459.2 15.3 %copy-start.9 = (f32[2,576,12,64]{1,3,2,0:T(8,128)S(1)}, f32[2,576,12,64]{1,3,2,0:T(8,128)}, u32[]{:S(2)}) copy-start(f32[2,576,12,64]{1,3,2,0:T(8,128)} %get-tuple-element.110) | copy-start | bytes 10616836
  503.5 293.1 %reduce-scatter.9.cloned.1.call-start = ((), (), s32[]{:S(2)}) async-start(), calls=%async_computation.10 | async-start | bytes 10616832 | tf_op jit(solution)/shard_map/reduce_scatter | solution.py:285
  516.7 446.5 %reduce-scatter.11.cloned.1.call-start = ((), (), s32[]{:S(2)}) async-start(), calls=%async_computation.11 | async-start | bytes 10616832 | tf_op jit(solution)/shard_map/reduce_scatter | solution.py:287
  528.3 504.8 %all-reduce.23.cloned.1.call-start = ((), (), s32[]{:S(2)}) async-start(), calls=%async_computation.12 | async-start | bytes 3538944 | tf_op jit(solution)/shard_map/psum | solution.py:293
  534.1 17.9 %slice-start = ((s8[7077888]{0:T(1024)(128)(4,1)}), s8[4194304]{0:T(1024)(128)(4,1)S(1)}, s32[]{:S(2)}) async-start(s8[7077888]{0:T(1024)(128)(4,1)} %bitcast.186), calls=%async_computation.13 | async-start | bytes 8388608
  534.1 17.9 %slice-start.2 = ((s8[4718592]{0:T(1024)(128)(4,1)}), s8[4194304]{0:T(1024)(128)(4,1)S(1)}, s32[]{:S(2)}) async-start(s8[4718592]{0:T(1024)(128)(4,1)} %bitcast.194), calls=%async_computation.15 | async-start | bytes 8388608
  535.6 14.9 %copy-start.15 = (bf16[2,576,768]{2,1,0:T(8,128)(2,1)S(1)}, bf16[2,576,768]{2,1,0:T(8,128)(2,1)}, u32[]{:S(2)}) copy-start(bf16[2,576,768]{2,1,0:T(8,128)(2,1)} %copy.73) | copy-start | bytes 5308420
  535.6 14.9 %copy-start.16 = (bf16[2,576,768]{2,1,0:T(8,128)(2,1)S(1)}, bf16[2,576,768]{2,1,0:T(8,128)(2,1)}, u32[]{:S(2)}) copy-start(bf16[2,576,768]{2,1,0:T(8,128)(2,1)} %copy.72) | copy-start | bytes 5308420
  535.6 14.9 %copy-start.17 = (bf16[2,576,768]{2,1,0:T(8,128)(2,1)S(1)}, bf16[2,576,768]{2,1,0:T(8,128)(2,1)}, u32[]{:S(2)}) copy-start(bf16[2,576,768]{2,1,0:T(8,128)(2,1)} %copy.71) | copy-start | bytes 5308420
  535.6 16.4 %slice-start.1 = ((s8[7077888]{0:T(1024)(128)(4,1)}), s8[2883584]{0:T(1024)(128)(4,1)S(1)}, s32[]{:S(2)}) async-start(s8[7077888]{0:T(1024)(128)(4,1)} %bitcast.186), calls=%async_computation.14 | async-start | bytes 5767168
  535.6 16.4 %slice-start.3 = ((s8[4718592]{0:T(1024)(128)(4,1)}), s8[524288]{0:T(1024)(128)(4,1)S(1)}, s32[]{:S(2)}) async-start(s8[4718592]{0:T(1024)(128)(4,1)} %bitcast.194), calls=%async_computation.16 | async-start | bytes 1048576
  (48 other events, 316.6 us)
Sparse Core Ops, SparseCore 0:
  10.8 68.5 all-gather.5
  82.1 40.0 all-gather.7
  125.0 78.6 all-gather.9
  206.2 78.1 all-gather.11
  337.0 66.3 reduce-scatter.6
  503.6 126.3 reduce-scatter.4
  634.0 162.5 reduce-scatter.8
  800.6 162.5 reduce-scatter.10
  967.1 45.6 all-reduce.22
where the time goes:
time: 1060 us; the launch traced here: 1050 us
  waiting for transfers between devices  398 us (38%)
  matrix products  244 us (23%)
  other arithmetic  206 us (19%)
  blocking collectives  110 us (10%)
  local copies, waits for them, and re-layouts  67.6 us (6%)
  between operations  19.3 us (2%)
    reduce_scatter x1, waiting for transfers between devices, on_device(): lax.psum_scatter(grads[9], 'dp', scatter_dimension=0, tiled=True)  165 us
    reduce_scatter x1, waiting for transfers between devices, on_device(): lax.psum_scatter(grads[11], 'dp', scatter_dimension=0, tiled=True)  164 us
    unnamed x2, blocking collectives  77.5 us
    reduce_scatter x1, waiting for transfers between devices, on_device(): lax.psum_scatter(grads[2], 'dp', scatter_dimension=0, tiled=True)  68.5 us
    dot_general x4, matrix products, weighted_outer(): jnp.einsum('isd,isf->df', left_rows, right_rows, preferred_element_type=j...  37.8 us
    convert_element_type x1, other arithmetic, on_device(): hidden = gelu_value.astype(bf16)  35.6 us
    unnamed x118, local copies, waits for them, and re-layouts  28.9 us
    convert_element_type x2, other arithmetic, attend_backward(): scores_low = grad_scores.astype(jnp.bfloat16)  28.3 us
  transfers between devices with their start and end apart: 9, of which 3 were waited for; matrix products, arithmetic and copies ran while one was open for 44% of the time, Pallas kernels for 0%

commit v1 on v0

v1 whole, which is shorter than its diff:
```python
import functools
import math

import jax
import jax.numpy as jnp
from jax import lax
from jax.experimental import pallas as pl
from jax.experimental.pallas import tpu as pltpu
from jax.sharding import PartitionSpec as P

HEADS = 12
HD = 64
SIDE_S = 14
SIDE_M = 20
SIDE_L = 24
SLOT = 576
D = 768
FF = 3072
LN_EPS = 1e-06
MASK_FILL = -1e30
BF = jnp.bfloat16
F32 = jnp.float32
NT = (((1,), (1,)), ((), ()))
NN = (((1,), (0,)), ((), ()))
TN = (((0,), (0,)), ((), ()))
R_G1, R_S1, R_QB, R_FR, R_OB, R_G2, R_S2, R_UB, R_DB, R_ALL = 0, 1, 2, 5, 6, 7, 8, 9, 13, 16
LOG2E = math.log2(math.e)


def dot(a, b, dims, precision=None):
    return lax.dot_general(a, b, dims, preferred_element_type=F32, precision=precision)


def vm(n):
    return [pl.BlockSpec(memory_space=pltpu.VMEM)] * n


def norm_stats(x):
    mean = jnp.mean(x, axis=-1, keepdims=True)
    cen = x - mean
    var = jnp.mean(cen * cen, axis=-1, keepdims=True)
    inv = lax.rsqrt(var + LN_EPS)
    return cen * inv, inv


def sincos(x):
    n = jnp.floor(x * (2.0 / math.pi) + 0.5)
    r = x - n * 1.5703125
    r = r - n * 4.837512969970703125e-4
    r = r - n * 7.54978995489188216e-8
    q = n.astype(jnp.int32)
    r2 = r * r
    s = r + r * r2 * (-1.6666654611e-1 + r2 * (8.3321608736e-3 + r2 * -1.9515295891e-4))
    c = 1.0 - 0.5 * r2 + r2 * r2 * (
        4.166664568298827e-2 + r2 * (-1.388731625493765e-3 + r2 * 2.443315711809948e-5)
    )
    odd = (q & 1) == 1
    ss = jnp.where(odd, c, s)
    cc = jnp.where(odd, s, c)
    ss = jnp.where((q & 2) == 2, -ss, ss)
    cc = jnp.where(((q + 1) & 2) == 2, -cc, cc)
    return ss, cc


def gelu_pair(x):
    z = jnp.abs(x) * math.sqrt(0.5)
    t = 1.0 / (1.0 + 0.5 * z)
    poly = 0.17087277
    for c in (
        -0.82215223,
        1.48851587,
        -1.13520398,
        0.27886807,
        -0.18628806,
        0.09678418,
        0.37409196,
        1.00002368,
        -1.26551223,
    ):
        poly = poly * t + c
    zz = z * z
    half = 0.5 * t * jnp.exp2((poly - zz) * LOG2E)
    cdf = jnp.where(x < 0, half, 1.0 - half)
    dens = math.sqrt(0.5 / math.pi) * jnp.exp2(zz * -LOG2E)
    return x * cdf, cdf + x * dens


def swap_halves(x):
    width = x.shape[-1]
    lane = lax.broadcasted_iota(jnp.int32, (1, width), 1)
    ahead = pltpu.roll(x, width - HD // 2, 1)
    behind = pltpu.roll(x, HD // 2, 1)
    return jnp.where(lane % HD < HD // 2, ahead, behind)


def half_sign(width):
    lane = lax.broadcasted_iota(jnp.int32, (1, width), 1)
    return jnp.where(lane % HD < HD // 2, 1.0, -1.0).astype(F32)


def patch_columns(side_ref, image):
    side = side_ref[image].astype(F32)
    slot = lax.broadcasted_iota(jnp.int32, (SLOT, 128), 0).astype(F32)
    row = jnp.floor((slot + 0.5) / side)
    col = slot - row * side
    valid = slot < side * side
    return col, row, valid


def spread(which):
    src = lax.broadcasted_iota(jnp.int32, (D, D), 0)
    lane = lax.broadcasted_iota(jnp.int32, (D, D), 1)
    want = which * (D // 2) + (lane // HD) * (HD // 2) + lane % (HD // 2)
    return (src == want).astype(BF)


def qkv_kernel(images, side_ref, x_ref, small_ref, w_ref, qkv_ref, norm_ref, cos_ref, sin_ref):
    gain = small_ref[R_G1 : R_G1 + 1]
    shift = small_ref[R_S1 : R_S1 + 1]
    freq = jnp.broadcast_to(small_ref[R_FR : R_FR + 1], (8, D)).astype(BF)
    fcol = dot(freq, spread(0), NN)[0:1]
    frow = dot(freq, spread(1), NN)[0:1]
    for i in range(images):
        rows = pl.ds(i * SLOT, SLOT)
        unit, _ = norm_stats(x_ref[rows])
        norm_ref[rows] = (unit * gain + shift).astype(BF)
        col, row, _ = patch_columns(side_ref, i)
        for j in range(D // 128):
            lanes = pl.ds(j * 128, 128)
            sn, cs = sincos(col * fcol[:, j * 128 : (j + 1) * 128] + row * frow[:, j * 128 : (j + 1) * 128])
            cos_ref[rows, lanes] = cs
            sin_ref[rows, lanes] = sn * -half_sign(128)

    def block(step, _):
        i, j = step // 9, step % 9
        rows = pl.ds(pl.multiple_of(i * SLOT, SLOT), SLOT)
        lanes = pl.ds(pl.multiple_of(j * 256, 256), 256)
        inner = pl.ds(pl.multiple_of((j % 3) * 256, 256), 256)
        raw = dot(norm_ref[rows], w_ref[:, lanes], NN) + small_ref[pl.ds(R_QB + j // 3, 1), inner]

        @pl.when(j < 6)
        def _():
            turned = raw * cos_ref[rows, inner] + swap_halves(raw) * sin_ref[rows, inner]
            qkv_ref[rows, lanes] = turned.astype(BF)

        @pl.when(j >= 6)
        def _():
            qkv_ref[rows, lanes] = raw.astype(BF)

        return 0

    lax.fori_loop(0, images * 9, block, 0)


def mask_column(side_ref, image):
    side = side_ref[image]
    slot = lax.broadcasted_iota(jnp.int32, (SLOT, 1), 0)
    return jnp.where(slot < side * side, 0.0, MASK_FILL).astype(F32)


def attend_step(step, side_ref, qkv_ref, ctx_ref, lse_ref):
    i, j = step // (HEADS // 2), step % (HEADS // 2)
    rows = pl.ds(pl.multiple_of(i * SLOT, SLOT), SLOT)
    c = pl.multiple_of(j * 128, 128)
    q = qkv_ref[rows, pl.ds(c, 128)]
    k = qkv_ref[rows, pl.ds(c + D, 128)]
    v = qkv_ref[rows, pl.ds(c + 2 * D, 128)]
    lane = lax.broadcasted_iota(jnp.int32, (1, 128), 1)
    mask = mask_column(side_ref, i)
    outs, logs = [], []
    for h in range(2):
        qm = jnp.where(lane // HD == h, q, jnp.zeros_like(q))
        s = dot(k, qm, NT) * (LOG2E / math.sqrt(HD)) + mask
        top = jnp.max(s, axis=0, keepdims=True)
        e = jnp.exp2(s - top)
        total = jnp.sum(e, axis=0, keepdims=True)
        p = (e * (1.0 / total)).astype(BF)
        outs.append(dot(p, v, TN))
        logs.append(top + jnp.log2(total))
    ctx_ref[rows, pl.ds(c, 128)] = jnp.where(lane < HD, outs[0], outs[1]).astype(BF)
    lse_ref[step] = jnp.concatenate(logs + [jnp.zeros((6, SLOT), F32)], axis=0)


def attend_kernel(images, side_ref, qkv_ref, ctx_ref, lse_ref):
    def body(step, _):
        attend_step(step, side_ref, qkv_ref, ctx_ref, lse_ref)
        return 0

    lax.fori_loop(0, images * HEADS // 2, body, 0)


def mlp_kernel(
    tiles,
    tm,
    wsteps,
    side_ref,
    scale_ref,
    x_ref,
    cot_ref,
    ctx_ref,
    small_ref,
    wo_ref,
    wu_ref,
    wd_ref,
    act_ref,
    gm_ref,
    gctx_ref,
    gd_ref,
    gu_ref,
    go_ref,
    gs_ref,
    hid_ref,
    gp_ref,
    n2_ref,
    bl_ref,
    al_ref,
    ctxall_ref,
):
    step = pl.program_id(0)

    @pl.when(step == 0)
    def _():
        gs_ref[...] = jnp.zeros_like(gs_ref)

    @pl.when(step < tiles)
    def _():
        per_image = SLOT // tm
        side = side_ref[step // per_image]
        slot = lax.broadcasted_iota(jnp.int32, (tm, 1), 0) + (step % per_image) * tm
        valid = slot < side * side
        rows = pl.ds(pl.multiple_of(step * tm, tm), tm)
        ctx = ctx_ref[...]
        ctxall_ref[rows] = ctx
        middle = x_ref[...] + (dot(ctx, wo_ref[...], NN) + small_ref[R_OB : R_OB + 1])
        unit, inv = norm_stats(middle)
        gain = small_ref[R_G2 : R_G2 + 1]
        n2_ref[rows] = (unit * gain + small_ref[R_S2 : R_S2 + 1]).astype(BF)
        gbranch = jnp.where(valid, cot_ref[...], 0.0)
        low = gbranch.astype(BF)
        bl_ref[rows] = low

        def block(j, _):
            lanes = pl.ds(pl.multiple_of(j * 256, 256), 256)
            inner = pl.ds(pl.multiple_of((j % 3) * 256, 256), 256)
            pre = dot(n2_ref[rows], wu_ref[:, lanes], NN) + small_ref[pl.ds(R_UB + j // 3, 1), inner]
            back = dot(bl_ref[rows], wd_ref[lanes], NT)
            value, slope = gelu_pair(pre)
            hid_ref[rows, lanes] = value.astype(BF)
            gpre = (back * slope).astype(BF)
            gp_ref[rows, lanes] = gpre
            gs_ref[pl.ds(R_UB + j // 3, 1), inner] += jnp.sum(gpre.astype(F32), axis=0, keepdims=True)
            return 0

        lax.fori_loop(0, FF // 256, block, 0)
        branch = dot(hid_ref[rows], wd_ref[...], NN) + small_ref[R_DB : R_DB + 1]
        act_ref[...] = jnp.where(valid, middle + branch, 0.0)
        gn = dot(gp_ref[rows], wu_ref[...], NT)
        gs_ref[R_G2 : R_G2 + 1] += jnp.sum(gn * unit, axis=0, keepdims=True)
        gs_ref[R_S2 : R_S2 + 1] += jnp.sum(gn, axis=0, keepdims=True)
        a = gn * gain
        ma = jnp.mean(a, axis=-1, keepdims=True)
        mu = jnp.mean(a * unit, axis=-1, keepdims=True)
        gm = gbranch + inv * (a - ma - unit * mu)
        gm_ref[...] = gm
        al = gm.astype(BF)
        al_ref[rows] = al
        gs_ref[R_OB : R_OB + 1] += jnp.sum(al.astype(F32), axis=0, keepdims=True)
        gs_ref[R_DB : R_DB + 1] += jnp.sum(low.astype(F32), axis=0, keepdims=True)
        gctx_ref[...] = dot(al, wo_ref[...], NT).astype(BF)

    @pl.when(step >= tiles)
    def _():
        scale = scale_ref[0]
        width = FF // wsteps
        lanes = pl.ds(pl.multiple_of((step - tiles) * width, width), width)
        gd_ref[...] = (dot(hid_ref[:, lanes], bl_ref[...], TN) * scale).astype(BF)
        gu_ref[...] = (dot(n2_ref[...], gp_ref[:, lanes], TN) * scale).astype(BF)

        @pl.when(step == tiles)
        def _():
            go_ref[...] = (dot(ctxall_ref[...], al_ref[...], TN) * scale).astype(BF)
            gs_ref[...] = gs_ref[...] * scale


def attend_back_step(step, side_ref, qkv_ref, gctx_ref, lse_ref, cos_ref, sin_ref, gproj_ref, gs_ref, gf_ref):
    i, j = step // (HEADS // 2), step % (HEADS // 2)
    rows = pl.ds(pl.multiple_of(i * SLOT, SLOT), SLOT)
    c = pl.multiple_of(j * 128, 128)
    q = qkv_ref[rows, pl.ds(c, 128)]
    k = qkv_ref[rows, pl.ds(c + D, 128)]
    v = qkv_ref[rows, pl.ds(c + 2 * D, 128)]
    go = gctx_ref[rows, pl.ds(c, 128)]
    lane = lax.broadcasted_iota(jnp.int32, (1, 128), 1)
    mask = mask_column(side_ref, i)
    lse = lse_ref[step]
    dq, dk, dv = [], [], []
    for h in range(2):
        mine = lane // HD == h
        qm = jnp.where(mine, q, jnp.zeros_like(q))
        gom = jnp.where(mine, go, jnp.zeros_like(go))
        s = dot(k, qm, NT) * (LOG2E / math.sqrt(HD)) + mask
        p = jnp.exp2(s - lse[h : h + 1])
        dp = dot(v, gom, NT)
        dv.append(dot(p.astype(BF), go, NN))
        t = p * dp
        ds = (t - p * jnp.sum(t, axis=0, keepdims=True)).astype(BF)
        dk.append(dot(ds, q, NN))
        dq.append(dot(ds, k, TN))
    first = lane < HD
    cs = cos_ref[rows, pl.ds(c, 128)]
    sn = sin_ref[rows, pl.ds(c, 128)]
    angle = None
    for n, (pair, rot) in enumerate(((dq, q), (dk, k))):
        e = jnp.where(first, pair[0], pair[1]) * (1.0 / math.sqrt(HD))
        other = swap_halves(e)
        back = (e * cs - other * sn).astype(BF)
        gproj_ref[rows, pl.ds(c + n * D, 128)] = back
        gs_ref[pl.ds(R_QB + n, 1), pl.ds(c, 128)] += jnp.sum(back.astype(F32), axis=0, keepdims=True)
        term = rot.astype(F32) * other
        angle = term if angle is None else angle + term
    gv = jnp.where(first, dv[0], dv[1]).astype(BF)
    gproj_ref[rows, pl.ds(c + 2 * D, 128)] = gv
    gs_ref[R_QB + 2 : R_QB + 3, pl.ds(c, 128)] += jnp.sum(gv.astype(F32), axis=0, keepdims=True)
    angle = angle * half_sign(128)
    col, row, _ = patch_columns(side_ref, i)
    gf_ref[0:1, pl.ds(c, 128)] += jnp.sum(angle * col, axis=0, keepdims=True)
    gf_ref[1:2, pl.ds(c, 128)] += jnp.sum(angle * row, axis=0, keepdims=True)


def freq_row(gf_ref):
    hi = lax.Precision.HIGHEST
    both = gf_ref[...]
    return (
        dot(both[0:8], spread(0).astype(F32), NT, hi)[0:1] + dot(both[0:8], spread(1).astype(F32), NT, hi)[1:2]
    )


def attend_back_kernel(
    images, side_ref, qkv_ref, gctx_ref, lse_ref, cos_ref, sin_ref, gproj_ref, gs_ref, gf_ref
):
    gs_ref[...] = jnp.zeros_like(gs_ref)
    gf_ref[...] = jnp.zeros_like(gf_ref)

    def body(step, _):
        attend_back_step(step, side_ref, qkv_ref, gctx_ref, lse_ref, cos_ref, sin_ref, gproj_ref, gs_ref, gf_ref)
        return 0

    lax.fori_loop(0, images * HEADS // 2, body, 0)
    gs_ref[R_FR : R_FR + 1] = freq_row(gf_ref)


def qkv_back_kernel(
    images, scale_ref, x_ref, norm_ref, gproj_ref, gm_ref, small_ref, w_ref, gs_in, gw_ref, gin_ref, gs_ref
):
    scale = scale_ref[0]

    def wblock(j, _):
        lanes = pl.ds(pl.multiple_of(j * 256, 256), 256)
        gw_ref[:, lanes] = (dot(norm_ref[...], gproj_ref[:, lanes], TN) * scale).astype(BF)
        return 0

    lax.fori_loop(0, 9, wblock, 0)
    gain = small_ref[R_G1 : R_G1 + 1]
    gs_ref[...] = gs_in[...]
    for i in range(images):
        rows = pl.ds(i * SLOT, SLOT)
        unit, inv = norm_stats(x_ref[rows])
        gn = dot(gproj_ref[rows], w_ref[...], NT)
        gs_ref[R_G1 : R_G1 + 1] += jnp.sum(gn * unit, axis=0, keepdims=True)
        gs_ref[R_S1 : R_S1 + 1] += jnp.sum(gn, axis=0, keepdims=True)
        a = gn * gain
        ma = jnp.mean(a, axis=-1, keepdims=True)
        mu = jnp.mean(a * unit, axis=-1, keepdims=True)
        gin_ref[rows] = gm_ref[rows] + inv * (a - ma - unit * mu)
    gs_ref[...] = gs_ref[...] * scale


def params(mb=56):
    return pltpu.CompilerParams(vmem_limit_bytes=mb << 20)


def place_rows(p, dp, vec):
    n = vec.shape[0]
    whole = jnp.tile(vec, dp)
    owner = jnp.arange(n * dp, dtype=jnp.int32) // n
    return jnp.where(owner == p, whole, 0.0).reshape(-1, D)


def on_device(
    images,
    cotangent,
    resolution,
    assignment,
    counts,
    ln1_gain,
    ln1_shift,
    qkv_weight,
    qkv_bias,
    rope_freqs,
    out_weight,
    out_bias,
    ln2_gain,
    ln2_shift,
    up_weight,
    up_bias,
    down_weight,
    down_bias,
):
    p = lax.axis_index("dp")
    dp = lax.axis_size("dp")
    n = images.shape[0]
    rows = n * SLOT
    x = images.reshape(rows, D)
    cot = cotangent.reshape(rows, D)
    side = jnp.where(resolution == 0, SIDE_S, jnp.where(resolution == 1, SIDE_M, SIDE_L)).astype(jnp.int32)
    group_total = counts.shape[0]
    cf = counts.astype(F32)
    picked = jnp.sum(jnp.where(assignment[0] == jnp.arange(group_total, dtype=jnp.int32), cf, 0.0))
    scale = group_total * picked / jnp.sum(cf) / math.sqrt(dp * n * SLOT)
    scale = scale.reshape(1)
    packed = jnp.concatenate(
        [
            place_rows(p, dp, v.astype(BF).astype(F32))
            for v in (ln1_gain, ln1_shift, qkv_bias, rope_freqs, out_bias, ln2_gain, ln2_shift, up_bias, down_bias)
        ]
        + [jnp.zeros((2, D), F32)],
        axis=0,
    )
    small = lax.psum(packed, "dp")
    wqkv = lax.all_gather(qkv_weight.astype(BF), "dp", axis=0, tiled=True)
    wo = lax.all_gather(out_weight.astype(BF), "dp", axis=0, tiled=True)
    wu = lax.all_gather(up_weight.astype(BF), "dp", axis=0, tiled=True)
    wd = lax.all_gather(down_weight.astype(BF), "dp", axis=0, tiled=True)

    sds = jax.ShapeDtypeStruct
    smem = pl.BlockSpec(memory_space=pltpu.SMEM)
    qkv, norm1, cos, sin = pl.pallas_call(
        functools.partial(qkv_kernel, n),
        out_shape=[sds((rows, 3 * D), BF), sds((rows, D), BF), sds((rows, D), F32), sds((rows, D), F32)],
        in_specs=[smem] + vm(3),
        out_specs=vm(4),
        compiler_params=params(),
        name="project",
    )(side, x, small, wqkv)
    ctx, lse = pl.pallas_call(
        functools.partial(attend_kernel, n),
        out_shape=[sds((rows, D), BF), sds((n * HEADS // 2, 8, SLOT), F32)],
        in_specs=[smem] + vm(1),
        out_specs=vm(2),
        compiler_params=params(),
        name="attend",
    )(side, qkv)

    tm = SLOT // 2
    tiles = rows // tm
    wsteps = 6
    once = dict(pipeline_mode=pl.Buffered(1))
    tile = lambda i: (jnp.minimum(i, tiles - 1), 0)
    full = lambda i: (0, 0)
    act, gm, gctx, gdown, gup, gout, gs_mlp = pl.pallas_call(
        functools.partial(mlp_kernel, tiles, tm, wsteps),
        grid=(tiles + wsteps,),
        out_shape=[
            sds((rows, D), F32),
            sds((rows, D), F32),
            sds((rows, D), BF),
            sds((FF, D), BF),
            sds((D, FF), BF),
            sds((D, D), BF),
            sds((R_ALL, D), F32),
        ],
        in_specs=[
            smem,
            smem,
            pl.BlockSpec((tm, D), tile),
            pl.BlockSpec((tm, D), tile),
            pl.BlockSpec((tm, D), tile),
            pl.BlockSpec((R_ALL, D), full, **once),
            pl.BlockSpec((D, D), full, **once),
            pl.BlockSpec((D, FF), full, **once),
            pl.BlockSpec((FF, D), full, **once),
        ],
        out_specs=[
            pl.BlockSpec((tm, D), tile),
            pl.BlockSpec((tm, D), tile),
            pl.BlockSpec((tm, D), tile),
            pl.BlockSpec((FF // wsteps, D), lambda i: (jnp.maximum(i - tiles, 0), 0)),
            pl.BlockSpec((D, FF // wsteps), lambda i: (0, jnp.maximum(i - tiles, 0))),
            pl.BlockSpec((D, D), full),
            pl.BlockSpec((R_ALL, D), full),
        ],
        scratch_shapes=[
            pltpu.VMEM((rows, FF), BF),
            pltpu.VMEM((rows, FF), BF),
            pltpu.VMEM((rows, D), BF),
            pltpu.VMEM((rows, D), BF),
            pltpu.VMEM((rows, D), BF),
            pltpu.VMEM((rows, D), BF),
        ],
        compiler_params=params(62),
        name="mlp",
    )(side, scale, x, cot, ctx, small, wo, wu, wd)

    gproj, gs_att = pl.pallas_call(
        functools.partial(attend_back_kernel, n),
        out_shape=[sds((rows, 3 * D), BF), sds((R_ALL, D), F32)],
        in_specs=[smem] + vm(5),
        out_specs=vm(2),
        scratch_shapes=[pltpu.VMEM((8, D), F32)],
        compiler_params=params(),
        name="attend_back",
    )(side, qkv, gctx, lse, cos, sin)
    gqkv, gin, gs_qkv = pl.pallas_call(
        functools.partial(qkv_back_kernel, n),
        out_shape=[sds((D, 3 * D), BF), sds((rows, D), F32), sds((R_ALL, D), F32)],
        in_specs=[smem] + vm(7),
        out_specs=vm(3),
        compiler_params=params(),
        name="project_back",
    )(scale, x, norm1, gproj, gm, small, wqkv, gs_att)

    def reduce(g):
        part = lax.psum_scatter(g, "dp", scatter_dimension=0, tiled=True)
        return lax.psum(part, "group").astype(F32)

    gs = lax.psum(gs_mlp + gs_qkv, ("group", "dp"))

    def own(first, count):
        flat = gs[first : first + count].reshape(dp, -1)
        return lax.dynamic_index_in_dim(flat, p, 0, keepdims=False)

    return (
        act.reshape(images.shape),
        gin.reshape(images.shape),
        own(R_G1, 1),
        own(R_S1, 1),
        reduce(gqkv),
        own(R_QB, 3),
        own(R_FR, 1),
        reduce(gout),
        own(R_OB, 1),
        own(R_G2, 1),
        own(R_S2, 1),
        reduce(gup),
        own(R_UB, 4),
        reduce(gdown),
        own(R_DB, 1),
    )


def solution(mesh):
    batch = P(("group", "dp"), None, None)
    per_image = P(("group", "dp"))
    vec, mat = P("dp"), P("dp", None)
    return jax.shard_map(
        on_device,
        mesh=mesh,
        in_specs=(batch, batch, per_image, per_image, P(), vec, vec, mat, vec, vec, mat, vec, vec, vec, mat, vec, mat, vec),
        out_specs=(batch, batch, vec, vec, mat, vec, vec, mat, vec, vec, vec, mat, vec, mat, vec),
        check_vma=False,
    )
```

time: 1060 us -> 769 us (0.73); the launches traced: 1050 us -> 769 us
  matrix products: 244 us -> 0 us
  Pallas kernels: 0 us -> 199 us
  other arithmetic: 206 us -> 15 us
  local copies, waits for them, and re-layouts: 67.6 us -> 6.29 us
  waiting for transfers between devices: 398 us -> 451 us
  blocking collectives: 110 us -> 81.5 us
    dot_general x26 -> x0, matrix products: 244 us -> none  [the longest x4 37.8 us: weighted_outer(): jnp.einsum('isd,isf->df', left_rows, right_rows, preferred_element_type=j...]
    pallas_call x0 -> x5, Pallas kernels: none -> 199 us  [the longest x1 79.4 us: on_device(): pl.pallas_call(functools.partial(mlp_kernel, tiles, tm, wsteps), grid=(ti...]
    all_gather x4, waiting for transfers between devices: 0.07 us -> 168 us  [the longest x1 80.7 us: on_device(): wd = lax.all_gather(down_weight.astype(BF), 'dp', axis=0, tiled=True)]
    reduce_scatter x4, waiting for transfers between devices: 398 us -> 238 us  [reduce(): part = lax.psum_scatter(g, 'dp', scatter_dimension=0, tiled=True)]
    convert_element_type x42 -> x17, other arithmetic: 116 us -> 13.7 us  [the longest x4 6.95 us: reduce(): return lax.psum(part, 'group').astype(F32)]
    unnamed x2 -> x0, blocking collectives: 77.5 us -> none
    psum x1 -> x2, blocking collectives: 6.4 us -> 81.5 us  [the longest x1 41 us: on_device(): small = lax.psum(packed, 'dp')]
    psum x1, waiting for transfers between devices: 0.01 us -> 43.6 us  [reduce(): return lax.psum(part, 'group').astype(F32)]
  transfers between devices with their start and end apart: 9 -> 9, of which waited for: 3 -> 7; matrix products, arithmetic and copies ran while one was open for 44% -> 2% of each run, Pallas kernels for 0% -> 16%
where the time goes in v1:
time: 769 us
  waiting for transfers between devices  451 us (59%)
  Pallas kernels  199 us (26%)
  blocking collectives  81.5 us (11%)
  between operations  15.6 us (2%)
  other arithmetic  15 us (2%)
    reduce_scatter x4, waiting for transfers between devices, reduce(): part = lax.psum_scatter(g, 'dp', scatter_dimension=0, tiled=True)  238 us
    all_gather x1, waiting for transfers between devices, on_device(): wd = lax.all_gather(down_weight.astype(BF), 'dp', axis=0, tiled=True)  80.7 us
    pallas_call x1, Pallas kernels, on_device(): pl.pallas_call(functools.partial(mlp_kernel, tiles, tm, wsteps), grid=(ti...  79.4 us
    all_gather x1, waiting for transfers between devices, on_device(): wu = lax.all_gather(up_weight.astype(BF), 'dp', axis=0, tiled=True)  66.5 us
    psum x1, waiting for transfers between devices, reduce(): return lax.psum(part, 'group').astype(F32)  43.6 us
    pallas_call x1, Pallas kernels, on_device(): pl.pallas_call(functools.partial(attend_back_kernel, n), out_shape=[sds((...  42 us
    psum x1, blocking collectives, on_device(): small = lax.psum(packed, 'dp')  41 us
    psum x1, blocking collectives, on_device(): gs = lax.psum(gs_mlp + gs_qkv, ('group', 'dp'))  40.5 us
  transfers between devices with their start and end apart: 9, of which 7 were waited for; matrix products, arithmetic and copies ran while one was open for 2% of the time, Pallas kernels for 16%

profile of v1, /device:TPU:0, one launch (start us, length us, event | category | flops | bytes accessed | tf_op | source)
XLA Modules:
  0.0 768.5 jit_solution(6275816219972940314)
XLA Ops:
  7.4 2.1 convert_element_type.100
  9.5 1.6 convert_element_type.101
  11.2 2.2 convert_element_type.102
  13.5 0.9 convert_element_type.103
  17.5 41.0 %psum.42.small_ref = f32[16,768]{1,0:T(8,128)} all-reduce(f32[16,768]{1,0:T(8,128)S(1)} %concatenate.3), channel_id=1, replica_groups=mesh['group'=4,'dp'=8] {'dp'}, use_global_device_ids=true, to_apply=%region_2.3 | all-reduce | flops 12288 | bytes 98304 | tf_op jit(solution)/shard_map/psum | solution.py:429
  59.0 20.8 %all-gather.5.cloned.1.call-done.w_ref = bf16[768,2304]{1,0:T(8,128)(2,1)} async-done(((bf16[96,2304]{1,0:T(8,128)(2,1)}), bf16[768,2304]{1,0:T(8,128)(2,1)}) %all-gather.5.cloned.1.call-update) | async-done | bytes 3538960 | tf_op jit(solution)/shard_map/all_gather | solution.py:430
  79.8 31.6 %project.1 = (bf16[1152,2304]{1,0:T(8,128)(2,1)}, bf16[1152,768]{1,0:T(8,128)(2,1)}, f32[1152,768]{1,0:T(8,128)}, f32[1152,768]{1,0:T(8,128)}) custom-call(s32[2]{0:T(128)} %compare_select_fusion.2.side_ref, f32[1152,768]{1,0:T(8,128)} %bitcast.21, f32[16,768]{1,0:T(8,128)} %psum.42.small_ref, bf16[768,2304]{1,0:T(8,128)(2,1)} %all-gather.5.cloned.1.call-done.w_ref), custom_call_target="tpu_custom_call" | custom-call | tf_op jit(solution)/shard_map/project/pallas_call | solution.py:437
  111.3 25.8 %attend.1 = (bf16[1152,768]{1,0:T(8,128)(2,1)}, f32[12,8,576]{2,1,0:T(8,128)}) custom-call(s32[2]{0:T(128)} %compare_select_fusion.2.side_ref, bf16[1152,2304]{1,0:T(8,128)(2,1)} %get-tuple-element.33.qkv_ref), custom_call_target="tpu_custom_call" | custom-call | tf_op jit(solution)/shard_map/attend/pallas_call | solution.py:445
  137.2 66.5 %all-gather.9.cloned.1.call-done.wu_ref = bf16[768,3072]{1,0:T(8,128)(2,1)} async-done(((bf16[96,3072]{1,0:T(8,128)(2,1)}), bf16[768,3072]{1,0:T(8,128)(2,1)}) %all-gather.9.cloned.1.call-update) | async-done | bytes 4718608 | tf_op jit(solution)/shard_map/all_gather | solution.py:432
  203.7 80.7 %all-gather.11.cloned.1.call-done.wd_ref = bf16[3072,768]{1,0:T(8,128)(2,1)} async-done(((bf16[384,768]{1,0:T(8,128)(2,1)}), bf16[3072,768]{1,0:T(8,128)(2,1)}) %all-gather.11.cloned.1.call-update) | async-done | bytes 4718608 | tf_op jit(solution)/shard_map/all_gather | solution.py:433
  284.4 79.4 %mlp.1 = (f32[1152,768]{1,0:T(8,128)}, f32[1152,768]{1,0:T(8,128)}, bf16[1152,768]{1,0:T(8,128)(2,1)}, bf16[3072,768]{1,0:T(8,128)(2,1)}, bf16[768,3072]{1,0:T(8...) custom-call(s32[2]{0:T(128)} %compare_select_fusion.2.side_ref, f32[1]{0:T(128)} %bitcast.1.scale_ref, ...), custom_call_target="tpu_custom_call" | custom-call | tf_op jit(solution)/shard_map/mlp/pallas_call | solution.py:460
  363.9 42.0 %attend_back.1 = (bf16[1152,2304]{1,0:T(8,128)(2,1)}, f32[16,768]{1,0:T(8,128)}) custom-call(s32[2]{0:T(128)} %compare_select_fusion.2.side_ref, bf16[1152,2304]{1,0:T(8,128)(2,1)} %get-tuple-element.33.qkv_ref, bf16[1152,768]{1,0:T(8,128)(2,1)} %get-tuple-element.37.gctx_ref, f32[12,8,576]{2,1,0:T(8,128)} %get-tuple-element.38.lse_ref, ...), custom_call_target="tpu_custom_call" | custom-call | tf_op jit(solution)/shard_map/attend_back/pallas_call | solution.py:504
  405.9 19.9 %project_back.1 = (bf16[768,2304]{1,0:T(8,128)(2,1)}, f32[1152,768]{1,0:T(8,128)}, f32[16,768]{1,0:T(8,128)}) custom-call(f32[1]{0:T(128)} %bitcast.1.scale_ref, f32[1152,768]{1,0:T(8,128)} %bitcast.23, bf16[1152,768]{1,0:T(8,128)(2,1)} %get-tuple-element.36.norm_ref, bf16[1152,2304]{1,0:T(8,128)(2,1)} %get-tuple-element.41.gproj_ref, ...), custom_call_target="tpu_custom_call" | custom-call | tf_op jit(solution)/shard_map/project_back/pallas_call | solution.py:513
  425.8 0.7 reduce-scatter.9.cloned.1.call-update
  426.6 0.7 reduce-scatter.11.cloned.1.call-update
  427.4 40.5 %psum.43 = f32[16,768]{1,0:T(8,128)S(1)} all-reduce(f32[16,768]{1,0:T(8,128)S(1)} %add.79), channel_id=1, replica_groups=mesh['group'=4,'dp'=8] {'group','dp'}, use_global_device_ids=true, to_apply=%region_3.4 | all-reduce | flops 12288 | bytes 98304 | tf_op jit(solution)/shard_map/psum | solution.py:526
  468.0 40.6 %reduce-scatter.5.cloned.1.call-done = bf16[96,2304]{1,0:T(8,128)(2,1)} async-done(((bf16[768,2304]{1,0:T(8,128)(2,1)}), bf16[96,2304]{1,0:T(8,128)(2,1)}) %reduce-scatter.5.cloned.1.call-update) | async-done | bytes 442384 | tf_op jit(solution)/shard_map/reduce_scatter | solution.py:523
  508.7 98.5 %reduce-scatter.9.cloned.1.call-done = bf16[96,3072]{1,0:T(8,128)(2,1)} async-done(((bf16[768,3072]{1,0:T(8,128)(2,1)}), bf16[96,3072]{1,0:T(8,128)(2,1)}) %reduce-scatter.9.cloned.1.call-update) | async-done | bytes 589840 | tf_op jit(solution)/shard_map/reduce_scatter | solution.py:523
  607.2 98.9 %reduce-scatter.11.cloned.1.call-done = bf16[384,768]{1,0:T(8,128)(2,1)} async-done(((bf16[3072,768]{1,0:T(8,128)(2,1)}), bf16[384,768]{1,0:T(8,128)(2,1)}) %reduce-scatter.11.cloned.1.call-update) | async-done | bytes 589840 | tf_op jit(solution)/shard_map/reduce_scatter | solution.py:523
  711.4 43.6 %all-reduce.3.cloned.1.call-done = (bf16[96,2304]{1,0:T(8,128)(2,1)}, bf16[96,768]{1,0:T(8,128)(2,1)}, bf16[96,3072]{1,0:T(8,128)(2,1)}, bf16[384,768]{1,0:T(8,128)(2,1)}) async-done(((bf16[96,2304]{1,0:T(8,128)(2,1)}, bf16[96,768]{1,0:T(8,128)(2,1)}, bf16[96,3072]{1,0:T(8,128)(2,1)}, bf16[384,768]{1,0:T(8,128)(2,1)}), (bf16[96,2304]{1,0:T(8,128)(2,1)}, bf16[96,768]{1,0:T(8,128)(2,1)}, ...) | async-done | bytes 1769488 | tf_op jit(solution)/shard_map/psum | solution.py:524
  755.0 1.7 convert_element_type.105
  756.7 2.0 convert_element_type.104
  758.7 2.2 convert_element_type.106
  760.9 1.1 convert_element_type.107
  (109 shorter events, 8.1 us)
Async XLA Ops:
  7.2 6.3 copy-start
  7.2 7.2 copy-start.4
  7.2 7.2 copy-start.8
  7.2 7.3 copy-start.9
  7.2 7.4 copy-start.10
  7.2 7.5 copy-start.11
  7.2 7.6 copy-start.12
  7.3 7.7 %copy-start.13 = (f32[96]{0:T(128)S(1)}, f32[96]{0:T(128)}, u32[]{:S(2)}) copy-start(f32[96]{0:T(128)} %param.24) | copy-start | bytes 1156
  7.3 7.8 %copy-start.14 = (f32[96]{0:T(128)S(1)}, f32[96]{0:T(128)}, u32[]{:S(2)}) copy-start(f32[96]{0:T(128)} %param.23) | copy-start | bytes 1156
  7.3 7.9 %copy-start.5 = (f32[288]{0:T(512)S(1)}, f32[288]{0:T(512)}, u32[]{:S(2)}) copy-start(f32[288]{0:T(512)} %param.26) | copy-start | bytes 3460
  7.3 8.0 %copy-start.6 = (s32[4]{0:T(128)S(1)}, s32[4]{0:T(128)}, u32[]{:S(2)}) copy-start(s32[4]{0:T(128)} %param.22) | copy-start | bytes 52
  7.3 8.0 %copy-start.7 = (s32[2]{0:T(128)S(1)}, s32[2]{0:T(128)}, u32[]{:S(2)}) copy-start(s32[2]{0:T(128)} %param.21) | copy-start | bytes 28
  7.3 51.2 %copy-start.15 = (s32[2]{0:T(128)S(1)}, s32[2]{0:T(128)}, u32[]{:S(2)}) copy-start(s32[2]{0:T(128)} %param.20) | copy-start | bytes 28
  7.3 72.5 %all-gather.5.cloned.1.call-start = ((), (), s32[]{:S(2)}) async-start(), calls=%async_computation.4 | async-start | bytes 3981312 | tf_op jit(solution)/shard_map/all_gather | solution.py:430
  9.4 127.7 %all-gather.7.cloned.1.call-start = ((), (), s32[]{:S(2)}) async-start(), calls=%async_computation.5 | async-start | bytes 1327104 | tf_op jit(solution)/shard_map/all_gather | solution.py:431
  11.2 192.6 %all-gather.9.cloned.1.call-start = ((), (), s32[]{:S(2)}) async-start(), calls=%async_computation.6 | async-start | bytes 5308416 | tf_op jit(solution)/shard_map/all_gather | solution.py:432
  13.4 271.0 %all-gather.11.cloned.1.call-start = ((), (), s32[]{:S(2)}) async-start(), calls=%async_computation.7 | async-start | bytes 5308416 | tf_op jit(solution)/shard_map/all_gather | solution.py:433
  14.4 453.7 %reduce-scatter.7.cloned.1.call-start = ((), (), s32[]{:S(2)}) async-start(), calls=%async_computation.9 | async-start | bytes 1327104 | tf_op jit(solution)/shard_map/reduce_scatter | solution.py:523
  363.8 144.8 %reduce-scatter.5.cloned.1.call-start = ((), (), s32[]{:S(2)}) async-start(), calls=%async_computation.8 | async-start | bytes 3981312 | tf_op jit(solution)/shard_map/reduce_scatter | solution.py:523
  425.8 181.4 %reduce-scatter.9.cloned.1.call-start = ((), (), s32[]{:S(2)}) async-start(), calls=%async_computation.10 | async-start | bytes 5308416 | tf_op jit(solution)/shard_map/reduce_scatter | solution.py:523
  426.5 0.8 copy-start.2
  426.6 279.5 %reduce-scatter.11.cloned.1.call-start = ((), (), s32[]{:S(2)}) async-start(), calls=%async_computation.11 | async-start | bytes 5308416 | tf_op jit(solution)/shard_map/reduce_scatter | solution.py:523
  427.3 327.7 %all-reduce.3.cloned.1.call-start = ((), (), s32[]{:S(2)}) async-start(), calls=%async_computation.12 | async-start | bytes 3538944 | tf_op jit(solution)/shard_map/psum | solution.py:524
  755.0 5.9 copy-start.1
  (1 other events, 0.8 us)
Sparse Core Ops, SparseCore 0:
  10.9 68.8 all-gather.4
  82.5 39.6 all-gather.6
  125.0 78.6 all-gather.8
  206.3 78.0 all-gather.10
  364.0 62.1 reduce-scatter.6
  429.7 78.9 reduce-scatter.4
  512.3 94.8 reduce-scatter.8
  610.8 95.1 reduce-scatter.10
  708.6 46.3 all-reduce.2
